TPU v7x, 32 devices: a whole 2x2x4 slice. The times are simulated.
32 devices in a mesh: shard: 4 (over y, x), ctx: 4 (over z), tp: 2 (over core).
Axes of the slice: x: 2, y: 2, z: 4, core: 2. Of those that a mesh axis runs over, the one named last changes fastest.
Arguments:
- inputs: bfloat16 [4096, 1024], P(('shard', 'ctx')), may hold values from -6 to 6
- lengths: int32 [4, 3], P('shard'), may hold values from 1 to 768, 1024 in all within a row
- cotangent: bfloat16 [4096, 1024], P(('shard', 'ctx')), may hold values from -6 to 6
- w_qkv: bfloat16 [3, 1024, 1024], P(None, 'shard', 'tp'), may hold values from -0.1875 to 0.1875
- w_out: bfloat16 [1024, 1024], P('tp', 'shard'), may hold values from -0.5 to 0.5
- w_fc: bfloat16 [1024, 4096], P('shard', 'tp'), may hold values from -0.1875 to 0.1875
- w_proj: bfloat16 [4096, 1024], P('tp', 'shard'), may hold values from -0.09375 to 0.09375
- b_qv: float32 [2, 1024], P(None, 'tp'), may hold values from -3 to 3
- b_out: float32 [1024], replicated, may hold values from -2 to 2
- b_fc: float32 [4096], P('tp'), may hold values from -3 to 3
- b_proj: float32 [1024], replicated, may hold values from -2 to 2
- ln1_gain: float32 [1024], replicated, may hold values from 0.25 to 1.75
- ln1_bias: float32 [1024], replicated, may hold values from -2 to 2
- ln2_gain: float32 [1024], replicated, may hold values from 0.25 to 1.75
- ln2_bias: float32 [1024], replicated, may hold values from -2 to 2
Outputs:
- outputs: bfloat16 [4096, 1024], P(('shard', 'ctx'))
- grad_inputs: bfloat16 [4096, 1024], P(('shard', 'ctx'))
- grad_w_qkv: float32 [3, 1024, 1024], P(None, 'shard', 'tp')
- grad_w_out: float32 [1024, 1024], P('tp', 'shard')
- grad_w_fc: float32 [1024, 4096], P('shard', 'tp')
- grad_w_proj: float32 [4096, 1024], P('tp', 'shard')
- grad_b_qv: float32 [2, 1024], P(None, 'tp')
- grad_b_out: float32 [1024], replicated
- grad_b_fc: float32 [4096], P('tp')
- grad_b_proj: float32 [1024], replicated
- grad_ln1_gain: float32 [1024], replicated
- grad_ln1_bias: float32 [1024], replicated
- grad_ln2_gain: float32 [1024], replicated
- grad_ln2_bias: float32 [1024], replicated
Inputs may be any that keep to these rules, and one draw needn't show every extreme that they name: Each row holds the lengths of one shard's 3 sequences in order; they sum to 1024, and the largest is 768.
All inputs are finite; a program needn't handle non-finite values.
Results may differ from a plain program's by a relative error of at most 0.02.
Values may be sent and summed in bfloat16 or wider, within the bound.
A program may use at most 128 MiB of HBM per device.

v0:
```python
import jax
import jax.numpy as jnp
from jax import lax
from jax.sharding import PartitionSpec as P

HEAD_DIM = 64


def layer_norm(values, gain, shift):
    mean = jnp.mean(values, axis=-1, keepdims=True)
    centred = values - mean
    spread = jnp.mean(centred * centred, axis=-1, keepdims=True)
    return centred * lax.rsqrt(spread + 1e-05) * gain + shift


def gelu_tanh(values):
    return (
        0.5
        * values
        * (1.0 + jnp.tanh(0.7978845608028654 * (values + 0.044715 * values * values * values)))
    )


def segment_ids(lengths, count):
    ends = jnp.cumsum(lengths)
    places = jnp.arange(count, dtype=jnp.int32)
    return jnp.sum((places[:, None] >= ends[None, :]).astype(jnp.int32), axis=1)


def dot32(left, right):
    return jnp.dot(left, right, preferred_element_type=jnp.float32)


def on_device(
    inputs,
    lengths,
    cotangent,
    w_qkv,
    w_out,
    w_fc,
    w_proj,
    b_qv,
    b_out,
    b_fc,
    b_proj,
    ln1_gain,
    ln1_bias,
    ln2_gain,
    ln2_bias,
):
    bf = jnp.bfloat16
    f32 = jnp.float32
    rows = inputs.shape[0]
    parts = lax.axis_size("ctx")
    block = rows * parts
    local_width = b_qv.shape[1]
    local_heads = local_width // HEAD_DIM
    seg_all = segment_ids(lengths[0], block)
    first = lax.axis_index("ctx") * rows
    q_pos = first + jnp.arange(rows, dtype=jnp.int32)
    q_seg = lax.dynamic_slice_in_dim(seg_all, first, rows)
    wq_all, wo_all, wfc_all, wproj_all = (
        lax.all_gather(w_qkv, "shard", axis=1, tiled=True),
        lax.all_gather(w_out, "shard", axis=1, tiled=True),
        lax.all_gather(w_fc, "shard", axis=0, tiled=True),
        lax.all_gather(w_proj, "shard", axis=1, tiled=True),
    )
    x_f = inputs.astype(f32)
    normed1 = layer_norm(x_f, ln1_gain, ln1_bias).astype(bf)
    query = ((dot32(normed1, wq_all[0]) + b_qv[0]) * 0.125).astype(bf)
    key = dot32(normed1, wq_all[1]).astype(bf)
    value = (dot32(normed1, wq_all[2]) + b_qv[1]).astype(bf)
    q3 = query.reshape(rows, local_heads, HEAD_DIM)

    def allowed_for(start, count):
        k_pos = start + jnp.arange(count, dtype=jnp.int32)
        k_seg = lax.dynamic_slice_in_dim(seg_all, start, count)
        return (k_pos[None, :] <= q_pos[:, None]) & (k_seg[None, :] == q_seg[:, None])

    k_piece = lax.all_gather(key, "ctx", axis=0, tiled=True)
    v_piece = lax.all_gather(value, "ctx", axis=0, tiled=True)
    count = k_piece.shape[0]
    allowed = allowed_for(jnp.int32(0), count)
    scores = jnp.einsum(
        "rhd,nhd->hrn",
        q3,
        k_piece.reshape(count, local_heads, HEAD_DIM),
        preferred_element_type=f32,
    )
    weights = jnp.where(allowed[None], jnp.exp(scores), 0.0)
    total = jnp.sum(weights, axis=2)
    acc = jnp.einsum(
        "hrn,nhd->hrd",
        weights.astype(bf),
        v_piece.reshape(count, local_heads, HEAD_DIM),
        preferred_element_type=f32,
    )
    total, acc = (total, acc)
    log_total = jnp.log(total)
    attended = (acc / total[:, :, None]).transpose(1, 0, 2).reshape(rows, local_width).astype(bf)
    mixed = lax.psum(dot32(attended, wo_all).astype(jnp.bfloat16), "tp").astype(jnp.float32)
    hidden = x_f + mixed + b_out
    normed2 = layer_norm(hidden, ln2_gain, ln2_bias).astype(bf)
    pre = dot32(normed2, wfc_all) + b_fc
    act = gelu_tanh(pre).astype(bf)
    mlp_total = lax.psum(dot32(act, wproj_all).astype(jnp.bfloat16), "tp").astype(jnp.float32)
    outputs = (hidden + mlp_total + b_proj).astype(bf)
    wq_back, wo_back, wfc_back, wproj_back = (
        lax.all_gather(w_qkv, "shard", axis=1, tiled=True),
        lax.all_gather(w_out, "shard", axis=1, tiled=True),
        lax.all_gather(w_fc, "shard", axis=0, tiled=True),
        lax.all_gather(w_proj, "shard", axis=1, tiled=True),
    )
    grad_f = cotangent.astype(f32)
    g_bproj = jnp.sum(grad_f, axis=0)
    g_proj = dot32(act.T, cotangent)
    d_act = dot32(cotangent, wproj_back.T)
    gelu_back = jax.vjp(gelu_tanh, pre)[1]
    d_pre = gelu_back(d_act)[0]
    g_bfc = jnp.sum(d_pre, axis=0)
    d_pre_b = d_pre.astype(bf)
    g_fc = dot32(normed2.T, d_pre_b)
    d_normed2 = lax.psum(dot32(d_pre_b, wfc_back.T).astype(jnp.bfloat16), "tp").astype(jnp.float32)
    norm_back2 = jax.vjp(layer_norm, hidden, ln2_gain, ln2_bias)[1]
    d_norm2, g_ln2g, g_ln2b = norm_back2(d_normed2)
    d_hidden = grad_f + d_norm2
    g_bout = jnp.sum(d_hidden, axis=0)
    d_hidden_b = d_hidden.astype(bf)
    g_out = dot32(attended.T, d_hidden_b)
    d_attended = dot32(d_hidden_b, wo_back.T).astype(bf)
    da3 = d_attended.reshape(rows, local_heads, HEAD_DIM)
    at3 = attended.reshape(rows, local_heads, HEAD_DIM)
    delta = jnp.einsum("rhd,rhd->hr", da3, at3, preferred_element_type=f32)
    key_all, value_all = (
        lax.all_gather(key, "ctx", axis=0, tiled=True),
        lax.all_gather(value, "ctx", axis=0, tiled=True),
    )
    key_blocks = key_all.reshape(parts, rows, local_heads, HEAD_DIM)
    value_blocks = value_all.reshape(parts, rows, local_heads, HEAD_DIM)
    starts = jnp.arange(parts, dtype=jnp.int32) * rows

    def back_piece(d_query_acc, inputs_piece):
        k_piece, v_piece, start = inputs_piece
        allowed = allowed_for(start, rows)
        scores = jnp.einsum("rhd,nhd->hrn", q3, k_piece, preferred_element_type=f32)
        probs = jnp.where(allowed[None], jnp.exp(scores - log_total[:, :, None]), 0.0)
        d_v = jnp.einsum("hrn,rhd->nhd", probs.astype(bf), da3, preferred_element_type=f32)
        d_probs = jnp.einsum("rhd,nhd->hrn", da3, v_piece, preferred_element_type=f32)
        d_scores_b = (probs * (d_probs - delta[:, :, None])).astype(bf)
        d_query_acc = d_query_acc + jnp.einsum(
            "hrn,nhd->rhd", d_scores_b, k_piece, preferred_element_type=f32
        )
        d_k = jnp.einsum("hrn,rhd->nhd", d_scores_b, q3, preferred_element_type=f32)
        return (d_query_acc, (d_k.reshape(rows, local_width), d_v.reshape(rows, local_width)))

    zero_query = jnp.zeros((rows, local_heads, HEAD_DIM), f32)
    d_query_acc, (d_key_terms, d_value_terms) = lax.scan(
        back_piece, zero_query, (key_blocks, value_blocks, starts)
    )
    d_key, d_value = (
        lax.psum_scatter(
            d_key_terms.reshape(block, local_width).astype(jnp.bfloat16),
            "ctx",
            scatter_dimension=0,
            tiled=True,
        ).astype(jnp.float32),
        lax.psum_scatter(
            d_value_terms.reshape(block, local_width).astype(jnp.bfloat16),
            "ctx",
            scatter_dimension=0,
            tiled=True,
        ).astype(jnp.float32),
    )
    d_query = d_query_acc.reshape(rows, local_width) * 0.125
    g_bqv = jnp.stack([jnp.sum(d_query, axis=0), jnp.sum(d_value, axis=0)])
    d_query_b = d_query.astype(bf)
    d_key_b = d_key.astype(bf)
    d_value_b = d_value.astype(bf)
    g_qkv = jnp.stack(
        [dot32(normed1.T, d_query_b), dot32(normed1.T, d_key_b), dot32(normed1.T, d_value_b)]
    )
    d_local = (
        dot32(d_query_b, wq_back[0].T)
        + dot32(d_key_b, wq_back[1].T)
        + dot32(d_value_b, wq_back[2].T)
    )
    d_normed1 = lax.psum(d_local.astype(jnp.bfloat16), "tp").astype(jnp.float32)
    norm_back1 = jax.vjp(layer_norm, x_f, ln1_gain, ln1_bias)[1]
    d_norm1, g_ln1g, g_ln1b = norm_back1(d_normed1)
    grad_inputs = (d_hidden + d_norm1).astype(bf)
    part_qkv, part_out, part_fc, part_proj = (
        lax.psum_scatter(
            g_qkv.astype(jnp.bfloat16), "shard", scatter_dimension=1, tiled=True
        ).astype(jnp.float32),
        lax.psum_scatter(
            g_out.astype(jnp.bfloat16), "shard", scatter_dimension=1, tiled=True
        ).astype(jnp.float32),
        lax.psum_scatter(
            g_fc.astype(jnp.bfloat16), "shard", scatter_dimension=0, tiled=True
        ).astype(jnp.float32),
        lax.psum_scatter(
            g_proj.astype(jnp.bfloat16), "shard", scatter_dimension=1, tiled=True
        ).astype(jnp.float32),
    )
    sum_qkv, sum_out, sum_fc, sum_proj = (
        lax.psum(part_qkv.astype(jnp.bfloat16), "ctx").astype(jnp.float32),
        lax.psum(part_out.astype(jnp.bfloat16), "ctx").astype(jnp.float32),
        lax.psum(part_fc.astype(jnp.bfloat16), "ctx").astype(jnp.float32),
        lax.psum(part_proj.astype(jnp.bfloat16), "ctx").astype(jnp.float32),
    )
    small = lax.psum(
        (g_bqv, g_bout, g_bfc, g_bproj, g_ln1g, g_ln1b, g_ln2g, g_ln2b), ("shard", "ctx")
    )
    return (
        outputs,
        grad_inputs,
        sum_qkv,
        sum_out,
        sum_fc,
        sum_proj,
        small[0],
        small[1],
        small[2],
        small[3],
        small[4],
        small[5],
        small[6],
        small[7],
    )


def solution(mesh):
    in_specs = (
        P(("shard", "ctx"), None),
        P("shard", None),
        P(("shard", "ctx"), None),
        P(None, "shard", "tp"),
        P("tp", "shard"),
        P("shard", "tp"),
        P("tp", "shard"),
        P(None, "tp"),
        P(),
        P("tp"),
        P(),
        P(),
        P(),
        P(),
        P(),
    )
    out_specs = (
        P(("shard", "ctx"), None),
        P(("shard", "ctx"), None),
        P(None, "shard", "tp"),
        P("tp", "shard"),
        P("shard", "tp"),
        P("tp", "shard"),
        P(None, "tp"),
        P(),
        P("tp"),
        P(),
        P(),
        P(),
        P(),
        P(),
    )
    return jax.shard_map(
        on_device, mesh=mesh, in_specs=in_specs, out_specs=out_specs, check_vma=False
    )
```

profile of v0, /device:TPU:0, one launch (start us, length us, event | category | flops | bytes accessed | tf_op | source)
XLA Modules:
  0.0 772.6 jit_solution(15052894565088602509)
XLA Ops:
  11.4 45.1 %all-gather.7.cloned.1.call-done = bf16[3,1024,512]{2,1,0:T(8,128)(2,1)} async-done(((bf16[3,256,512]{2,1,0:T(8,128)(2,1)}), bf16[3,1024,512]{2,1,0:T(8,128)(2,1)}) %all-gather.7.cloned.1.call-update) | async-done | bytes 3145744 | tf_op jit(solution)/shard_map/all_gather | solution.py:63
  56.4 2.6 fusion.47
  59.2 2.4 convolution_convert_fusion.10
  64.8 22.4 %all-gather.11.cloned.1.call-done = bf16[1024,512]{1,0:T(8,128)(2,1)} async-done(((bf16[256,512]{1,0:T(8,128)(2,1)}), bf16[1024,512]{1,0:T(8,128)(2,1)}) %all-gather.11.cloned.1.call-update) | async-done | bytes 1048592 | tf_op jit(solution)/shard_map/all_gather | solution.py:81
  88.7 28.1 %all-gather.9.cloned.1.call-done = bf16[1024,512]{1,0:T(8,128)(2,1)} async-done(((bf16[256,512]{1,0:T(8,128)(2,1)}), bf16[1024,512]{1,0:T(8,128)(2,1)}) %all-gather.9.cloned.1.call-update) | async-done | bytes 1048592 | tf_op jit(solution)/shard_map/all_gather | solution.py:80
  118.2 2.1 fusion.21
  121.7 22.5 %all-gather.13.cloned.1.call-done = bf16[512,1024]{1,0:T(8,128)(2,1)} async-done(((bf16[512,256]{1,0:T(8,128)(2,1)}), bf16[512,1024]{1,0:T(8,128)(2,1)}) %all-gather.13.cloned.1.call-update) | async-done | bytes 1048592 | tf_op jit(solution)/shard_map/all_gather | solution.py:64
  144.2 2.5 convolution_convert_fusion.6
  148.2 17.4 %all-reduce.8.cloned.1.call-done = bf16[256,1024]{1,0:T(8,128)(2,1)} async-done(((bf16[256,1024]{1,0:T(8,128)(2,1)}), bf16[256,1024]{1,0:T(8,128)(2,1)}) %all-reduce.8.cloned.1.call-update) | async-done | bytes 524304 | tf_op jit(solution)/shard_map/psum | solution.py:101
  168.4 52.8 %all-gather.15.cloned.1.call-done = bf16[1024,2048]{1,0:T(8,128)(2,1)} async-done(((bf16[256,2048]{1,0:T(8,128)(2,1)}), bf16[1024,2048]{1,0:T(8,128)(2,1)}) %all-gather.15.cloned.1.call-update) | async-done | bytes 4194320 | tf_op jit(solution)/shard_map/all_gather | solution.py:65
  221.1 4.9 convolution_add_fusion
  226.0 49.4 %all-gather.17.cloned.1.call-done = bf16[2048,1024]{1,0:T(8,128)(2,1)} async-done(((bf16[2048,256]{1,0:T(8,128)(2,1)}), bf16[2048,1024]{1,0:T(8,128)(2,1)}) %all-gather.17.cloned.1.call-update) | async-done | bytes 4194320 | tf_op jit(solution)/shard_map/all_gather | solution.py:66
  275.4 7.6 fusion.86
  284.0 2.1 convolution_convert_fusion.7
  286.4 2.8 reshape.278
  289.2 1.9 copy.61
  291.2 2.8 reshape.279
  294.0 1.9 copy.62
  295.9 9.0 %all-reduce.10.cloned.1.call-done = bf16[256,1024]{1,0:T(8,128)(2,1)} async-done(((bf16[256,1024]{1,0:T(8,128)(2,1)}), bf16[256,1024]{1,0:T(8,128)(2,1)}) %all-reduce.10.cloned.1.call-update) | async-done | bytes 524304 | tf_op jit(solution)/shard_map/psum | solution.py:123
  306.5 1.8 fusion.56
  312.3 53.9 %while.15 = (s32[]{:T(128)}, f32[256,8,64]{0,2,1:T(8,128)}, bf16[4,256,512]{2,1,0:T(8,128)(2,1)}, bf16[4,256,512]{2,1,0:T(8,128)(2,1)}, bf16[4,256,8,64]{1,3,2,0...) while((s32[]{:T(128)}, f32[256,8,64]{0,2,1:T(8,128)}, ...), condition=%wide.region_13.14_spmd.clone, body=%wide.region_12.13_spmd.clone.sunk | while | flops 340197888 | bytes 15172017 | solution.py:157
  317.2 1.7 fusion.144
  318.9 2.1 fusion.145
  321.0 2.1 fusion.146
  330.5 1.7 fusion.144
  332.3 2.2 fusion.145
  334.5 2.1 fusion.146
  344.0 1.7 fusion.144
  345.8 2.2 fusion.145
  348.0 2.1 fusion.146
  357.5 1.7 fusion.144
  359.3 2.2 fusion.145
  361.5 2.1 fusion.146
  368.9 3.4 convolution_convert_fusion.1
  373.4 5.2 convolution_convert_fusion
  381.4 13.5 %reduce-scatter.9.cloned.1.call-done = bf16[256,512]{1,0:T(8,128)(2,1)} async-done(((bf16[1024,512]{1,0:T(8,128)(2,1)}), bf16[256,512]{1,0:T(8,128)(2,1)}) %reduce-scatter.9.cloned.1.call-update) | async-done | bytes 262160 | tf_op jit(solution)/shard_map/reduce_scatter | solution.py:167
  394.8 2.5 fusion.38
  397.4 26.0 %reduce-scatter.7.cloned.1.call-done = bf16[256,512]{1,0:T(8,128)(2,1)} async-done(((bf16[1024,512]{1,0:T(8,128)(2,1)}), bf16[256,512]{1,0:T(8,128)(2,1)}) %reduce-scatter.7.cloned.1.call-update) | async-done | bytes 262160 | tf_op jit(solution)/shard_map/reduce_scatter | solution.py:161
  425.1 2.0 pad_maximum_fusion
  427.2 5.2 convolution_convert_fusion.8
  435.7 17.1 %reduce-scatter.13.cloned.1.call-done = bf16[512,256]{1,0:T(8,128)(2,1)} async-done(((bf16[512,1024]{1,0:T(8,128)(2,1)}), bf16[512,256]{1,0:T(8,128)(2,1)}) %reduce-scatter.13.cloned.1.call-update) | async-done | bytes 262160 | tf_op jit(solution)/shard_map/reduce_scatter | solution.py:195
  452.8 55.4 %reduce-scatter.15.cloned.1.call-done = bf16[256,2048]{1,0:T(8,128)(2,1)} async-done(((bf16[1024,2048]{1,0:T(8,128)(2,1)}), bf16[256,2048]{1,0:T(8,128)(2,1)}) %reduce-scatter.15.cloned.1.call-update) | async-done | bytes 1048592 | tf_op jit(solution)/shard_map/reduce_scatter | solution.py:198
  508.2 55.6 %reduce-scatter.17.cloned.1.call-done = bf16[2048,256]{1,0:T(8,128)(2,1)} async-done(((bf16[2048,1024]{1,0:T(8,128)(2,1)}), bf16[2048,256]{1,0:T(8,128)(2,1)}) %reduce-scatter.17.cloned.1.call-update) | async-done | bytes 1048592 | tf_op jit(solution)/shard_map/reduce_scatter | solution.py:201
  563.8 46.8 %reduce-scatter.11.cloned.1.call-done = bf16[3,256,512]{2,1,0:T(8,128)(2,1)} async-done(((bf16[3,1024,512]{2,1,0:T(8,128)(2,1)}), bf16[3,256,512]{2,1,0:T(8,128)(2,1)}) %reduce-scatter.11.cloned.1.call-update) | async-done | bytes 786448 | tf_op jit(solution)/shard_map/reduce_scatter | solution.py:192
  610.8 22.1 %all-reduce.14.cloned.1.call-done = (bf16[256,1024]{1,0:T(8,128)(2,1)}, bf16[256,1024]{1,0:T(8,128)(2,1)}) async-done(((bf16[256,1024]{1,0:T(8,128)(2,1)}, bf16[256,1024]{1,0:T(8,128)(2,1)}), (bf16[256,1024]{1,0:T(8,128)(2,1)}, bf16[256,1024]{1,0:T(8,128)(2,1)})) %all-reduce.14.cloned.1.call-update) | async-done | bytes 1048592 | tf_op jit(solution)/shard_map/psum | solution.py:106
  636.1 82.1 %all-reduce = (f32[2,512]{1,0:T(2,128)}, f32[1024]{0:T(1024)}, f32[2048]{0:T(1024)}, f32[1024]{0:T(1024)}, f32[1024]{0:T(1024)}, /*index=5*/f32[1024]{0:T(1024)}, f32[1024]{0:T(1024)}, f32[1024]{0:T(1024)}) all-reduce(f32[2,512]{1,0:T(2,128)S(1)} %pad_maximum_fusion.1, ...), channel_id=1, replica_groups=mesh['shard'=4,'ctx'=4,'tp'=2] {'shard','ctx'}, use_global_device_ids=true, to_apply=%region_29.30 | all-reduce | flops 9216 | bytes 73728 | tf_op jit(solution)/shard_map/psum | solution.py:211
  719.7 39.9 %all-reduce.12.cloned.1.call-done = (bf16[3,256,512]{2,1,0:T(8,128)(2,1)}, bf16[512,256]{1,0:T(8,128)(2,1)}, bf16[256,2048]{1,0:T(8,128)(2,1)}, bf16[2048,256]{1,0:T(8,128)(2,1)}) async-done(((bf16[3,256,512]{2,1,0:T(8,128)(2,1)}, bf16[512,256]{1,0:T(8,128)(2,1)}, bf16[256,2048]{1,0:T(8,128)(2,1)}, bf16[2048,256]{1,0:T(8,128)(2,1)}), (bf16[3,256,512]{2,1,0:T(8,128)(2,1)}, bf16[512,256]{1,0:T(8,128)(2,1)}, ...) | async-done | bytes 3145744 | tf_op jit(solution)/shard_map/psum | solution.py:206
  759.6 2.6 convert_element_type.168
  (211 shorter events, 64.5 us)
Async XLA Ops:
  7.2 49.3 %all-gather.7.cloned.1.call-start = ((), (), s32[]{:S(2)}) async-start(), calls=%async_computation.6 | async-start | bytes 3932160 | tf_op jit(solution)/shard_map/all_gather | solution.py:63
  7.9 79.3 %all-gather.11.cloned.1.call-start = ((), (), s32[]{:S(2)}) async-start(), calls=%async_computation.8 | async-start | bytes 1310720 | tf_op jit(solution)/shard_map/all_gather | solution.py:81
  9.2 50.0 %copy-start = (bf16[256,1024]{1,0:T(8,128)(2,1)S(1)}, bf16[256,1024]{1,0:T(8,128)(2,1)}, u32[]{:S(2)}) copy-start(bf16[256,1024]{1,0:T(8,128)(2,1)} %param.17) | copy-start | bytes 1572868
  9.2 50.0 %copy-start.30 = (f32[1024]{0:T(1024)S(1)}, f32[1024]{0:T(1024)}, u32[]{:S(2)}) copy-start(f32[1024]{0:T(1024)} %param.28) | copy-start | bytes 12292
  9.2 50.0 %copy-start.35 = (f32[1024]{0:T(1024)S(1)}, f32[1024]{0:T(1024)}, u32[]{:S(2)}) copy-start(f32[1024]{0:T(1024)} %param.29) | copy-start | bytes 12292
  59.0 3.2 copy-start.36
  59.1 57.7 %all-gather.9.cloned.1.call-start = ((), (), s32[]{:S(2)}) async-start(), calls=%async_computation.7 | async-start | bytes 1310720 | tf_op jit(solution)/shard_map/all_gather | solution.py:80
  61.6 82.6 %all-gather.13.cloned.1.call-start = ((), (), s32[]{:S(2)}) async-start(), calls=%async_computation.9 | async-start | bytes 1310720 | tf_op jit(solution)/shard_map/all_gather | solution.py:64
  62.2 103.4 %all-reduce.8.cloned.1.call-start = ((), (), s32[]{:S(2)}) async-start(), calls=%async_computation.10 | async-start | bytes 1048576 | tf_op jit(solution)/shard_map/psum | solution.py:101
  121.7 26.4 %copy-start.11 = (bf16[256,8,64]{0,2,1:T(8,128)(2,1)}, bf16[256,8,64]{0,2,1:T(8,128)(2,1)S(1)}, u32[]{:S(2)}) copy-start(bf16[256,8,64]{0,2,1:T(8,128)(2,1)S(1)} %fusion.62) | copy-start | bytes 786436
  144.2 21.4 %copy-start.25 = (f32[1024]{0:T(1024)S(1)}, f32[1024]{0:T(1024)}, u32[]{:S(2)}) copy-start(f32[1024]{0:T(1024)} %param.25) | copy-start | bytes 12292
  146.7 74.4 %copy-start.28 = (f32[1024]{0:T(1024)S(1)}, f32[1024]{0:T(1024)}, u32[]{:S(2)}) copy-start(f32[1024]{0:T(1024)} %param.30) | copy-start | bytes 12292
  146.8 74.4 %copy-start.29 = (f32[1024]{0:T(1024)S(1)}, f32[1024]{0:T(1024)}, u32[]{:S(2)}) copy-start(f32[1024]{0:T(1024)} %param.31) | copy-start | bytes 12292
  146.8 74.4 %copy-start.34 = (f32[2048]{0:T(1024)S(1)}, f32[2048]{0:T(1024)}, u32[]{:S(2)}) copy-start(f32[2048]{0:T(1024)} %param.26) | copy-start | bytes 24580
  146.8 74.3 %all-gather.15.cloned.1.call-start = ((), (), s32[]{:S(2)}) async-start(), calls=%async_computation.11 | async-start | bytes 5242880 | tf_op jit(solution)/shard_map/all_gather | solution.py:65
  147.4 128.1 %all-gather.17.cloned.1.call-start = ((), (), s32[]{:S(2)}) async-start(), calls=%async_computation.12 | async-start | bytes 5242880 | tf_op jit(solution)/shard_map/all_gather | solution.py:66
  148.1 156.8 %all-reduce.10.cloned.1.call-start = ((), (), s32[]{:S(2)}) async-start(), calls=%async_computation.13 | async-start | bytes 1048576 | tf_op jit(solution)/shard_map/psum | solution.py:123
  165.6 55.5 %copy-start.2 = (bf16[256,1024]{1,0:T(8,128)(2,1)S(1)}, bf16[256,1024]{1,0:T(8,128)(2,1)}, u32[]{:S(2)}) copy-start(bf16[256,1024]{1,0:T(8,128)(2,1)} %all-reduce.8.cloned.1.call-done) | copy-start | bytes 1572868
  168.4 107.1 %copy-start.21 = (bf16[256,1024]{1,0:T(8,128)(2,1)S(1)}, bf16[256,1024]{1,0:T(8,128)(2,1)}, u32[]{:S(2)}) copy-start(bf16[256,1024]{1,0:T(8,128)(2,1)} %param.19) | copy-start | bytes 1572868
  275.4 8.6 %copy-start.33 = (bf16[1024,2048]{1,0:T(8,128)(2,1)S(1)}, bf16[1024,2048]{1,0:T(8,128)(2,1)}, u32[]{:S(2)}) copy-start(bf16[1024,2048]{1,0:T(8,128)(2,1)} %all-gather.15.cloned.1.call-done) | copy-start | bytes 12582916
  286.2 108.7 %reduce-scatter.9.cloned.1.call-start = ((), (), s32[]{:S(2)}) async-start(), calls=%async_computation.15 | async-start | bytes 1310720 | tf_op jit(solution)/shard_map/reduce_scatter | solution.py:167
  295.9 12.4 %copy-start.22 = (bf16[256,1024]{1,0:T(8,128)(2,1)S(1)}, bf16[256,1024]{1,0:T(8,128)(2,1)}, u32[]{:S(2)}) copy-start(bf16[256,1024]{1,0:T(8,128)(2,1)} %param.19) | copy-start | bytes 1572868
  304.9 3.4 copy-start.7
  306.5 3.4 copy-start.9
  312.3 4.1 copy-start.37
  323.1 2.5 copy-start.38
  325.7 4.1 copy-start.37
  336.6 2.5 copy-start.38
  339.2 4.1 copy-start.37
  350.1 2.5 copy-start.38
  352.7 4.1 copy-start.37
  366.2 57.2 %reduce-scatter.7.cloned.1.call-start = ((), (), s32[]{:S(2)}) async-start(), calls=%async_computation.14 | async-start | bytes 1310720 | tf_op jit(solution)/shard_map/reduce_scatter | solution.py:161
  366.2 2.7 copy-start.1
  366.3 2.7 copy-start.3
  366.3 2.7 copy-start.20
  366.8 86.0 %reduce-scatter.13.cloned.1.call-start = ((), (), s32[]{:S(2)}) async-start(), calls=%async_computation.17 | async-start | bytes 1310720 | tf_op jit(solution)/shard_map/reduce_scatter | solution.py:195
  368.9 139.3 %reduce-scatter.15.cloned.1.call-start = ((), (), s32[]{:S(2)}) async-start(), calls=%async_computation.18 | async-start | bytes 5242880 | tf_op jit(solution)/shard_map/reduce_scatter | solution.py:198
  372.4 191.4 %reduce-scatter.17.cloned.1.call-start = ((), (), s32[]{:S(2)}) async-start(), calls=%async_computation.19 | async-start | bytes 5242880 | tf_op jit(solution)/shard_map/reduce_scatter | solution.py:201
  378.6 232.0 %reduce-scatter.11.cloned.1.call-start = ((), (), s32[]{:S(2)}) async-start(), calls=%async_computation.16 | async-start | bytes 3932160 | tf_op jit(solution)/shard_map/reduce_scatter | solution.py:192
  427.2 205.8 %all-reduce.14.cloned.1.call-start = ((), (), s32[]{:S(2)}) async-start(), calls=%async_computation.21 | async-start | bytes 2097152 | tf_op jit(solution)/shard_map/psum | solution.py:106
  427.2 5.2 copy-start.10
  435.6 324.0 %all-reduce.12.cloned.1.call-start = ((), (), s32[]{:S(2)}) async-start(), calls=%async_computation.20 | async-start | bytes 6291456 | tf_op jit(solution)/shard_map/psum | solution.py:206
  610.6 25.5 %copy-start.31 = (f32[2048]{0:T(1024)S(1)}, f32[2048]{0:T(1024)}, u32[]{:S(2)}) copy-start(f32[2048]{0:T(1024)} %get-tuple-element.231) | copy-start | bytes 24580
  610.6 107.6 %copy-start.32 = (f32[1024]{0:T(1024)S(1)}, f32[1024]{0:T(1024)}, u32[]{:S(2)}) copy-start(f32[1024]{0:T(1024)} %param.27) | copy-start | bytes 12292
  632.9 85.3 %copy-start.8 = (bf16[256,1024]{1,0:T(8,128)(2,1)S(1)}, bf16[256,1024]{1,0:T(8,128)(2,1)}, u32[]{:S(2)}) copy-start(bf16[256,1024]{1,0:T(8,128)(2,1)} %get-tuple-element.230) | copy-start | bytes 1572868
  632.9 85.3 %copy-start.24 = (bf16[256,1024]{1,0:T(8,128)(2,1)S(1)}, bf16[256,1024]{1,0:T(8,128)(2,1)}, u32[]{:S(2)}) copy-start(bf16[256,1024]{1,0:T(8,128)(2,1)} %get-tuple-element.229) | copy-start | bytes 1572868
  759.6 2.6 copy-start.26
  759.6 3.4 copy-start.15
  (13 other events, 19.2 us)
Sparse Core Ops, SparseCore 0:
  9.8 46.5 all-gather.6
  59.2 27.9 all-gather.10
  89.4 27.3 all-gather.8
  118.4 25.7 all-gather.12
  147.0 18.5 all-reduce.7
  167.3 53.7 all-gather.14
  222.9 52.4 all-gather.16
  286.3 18.5 all-reduce.9
  366.3 28.4 reduce-scatter.8
  397.5 25.7 reduce-scatter.6
  426.3 26.4 reduce-scatter.12
  455.6 52.5 reduce-scatter.14
  511.2 52.5 reduce-scatter.16
  566.6 43.9 reduce-scatter.10
  613.4 19.4 all-reduce.13
  635.4 124.1 all-reduce.11
where the time goes:
time: 774 us; the launch traced here: 773 us
  waiting for transfers between devices  526 us (68%)
  matrix products  82.7 us (11%)
  blocking collectives  82.1 us (11%)
  local copies, waits for them, and re-layouts  30.8 us (4%)
  other arithmetic  27.4 us (4%)
  between operations  14.4 us (2%)
  loops' own time  8.03 us (1%)
    psum x1, blocking collectives, on_device(): lax.psum((g_bqv, g_bout, g_bfc, g_bproj, g_ln1g, g_ln1b, g_ln2g, g_ln2b),...  82.1 us
    reduce_scatter x1, waiting for transfers between devices, on_device(): lax.psum_scatter(g_proj.astype(jnp.bfloat16), 'shard', scatter_dimension=...  55.6 us
    reduce_scatter x1, waiting for transfers between devices, on_device(): lax.psum_scatter(g_fc.astype(jnp.bfloat16), 'shard', scatter_dimension=0,...  55.4 us
    all_gather x1, waiting for transfers between devices, on_device(): lax.all_gather(w_fc, 'shard', axis=0, tiled=True)  52.8 us
    all_gather x1, waiting for transfers between devices, on_device(): lax.all_gather(w_proj, 'shard', axis=1, tiled=True)  49.4 us
    dot_general x18, matrix products, dot32(): return jnp.dot(left, right, preferred_element_type=jnp.float32)  47.6 us
    reduce_scatter x1, waiting for transfers between devices, on_device(): lax.psum_scatter(g_qkv.astype(jnp.bfloat16), 'shard', scatter_dimension=1...  46.8 us
    all_gather x1, waiting for transfers between devices, on_device(): lax.all_gather(w_qkv, 'shard', axis=1, tiled=True)  45.1 us
  transfers between devices with their start and end apart: 16, of which 16 were waited for; matrix products, arithmetic and copies ran while one was open for 8% of the time, Pallas kernels for 0%

commit v1 on v0

--- a/solution.py
+++ b/solution.py
@@ -59,10 +59,25 @@
     first = lax.axis_index("ctx") * rows
     q_pos = first + jnp.arange(rows, dtype=jnp.int32)
     q_seg = lax.dynamic_slice_in_dim(seg_all, first, rows)
+
+    def build_slot(content, named_axis, row_dim):
+        prior = lax.axis_size(named_axis)
+        reply = lax.axis_index(named_axis)
+        local_part, arr_next = (prior, reply)
+        block_now, finding = (content, 1)
+        while finding < local_part:
+            low = tuple(((i, i ^ finding) for i in range(local_part)))
+            local_out = lax.ppermute(block_now, named_axis, low)
+            current_value = jnp.concatenate([block_now, local_out], axis=row_dim)
+            clean = jnp.concatenate([local_out, block_now], axis=row_dim)
+            block_now = jnp.where(arr_next & finding == 0, current_value, clean)
+            finding = 2 * finding
+        return block_now
+
     wq_all, wo_all, wfc_all, wproj_all = (
         lax.all_gather(w_qkv, "shard", axis=1, tiled=True),
         lax.all_gather(w_out, "shard", axis=1, tiled=True),
-        lax.all_gather(w_fc, "shard", axis=0, tiled=True),
+        build_slot(w_fc, "shard", 0),
         lax.all_gather(w_proj, "shard", axis=1, tiled=True),
     )
     x_f = inputs.astype(f32)

time: 774 us -> 813 us (1.050)
  waiting for transfers between devices: 526 us -> 543 us
  matrix products: 82.7 us -> 90.9 us
    ppermute x0 -> x2, waiting for transfers between devices: none -> 99.4 us  [build_slot(): local_out = lax.ppermute(block_now, named_axis, low)]
    all_gather x1, waiting for transfers between devices: 49.4 us -> 0.01 us  [on_device(): lax.all_gather(w_proj, 'shard', axis=1, tiled=True)]
    psum x1, waiting for transfers between devices: 17.4 us -> 0.01 us  [on_device(): lax.psum(dot32(attended, wo_all).astype(jnp.bfloat16), 'tp')]
    all_gather x1, waiting for transfers between devices: 52.8 us -> 38.4 us  [on_device(): lax.all_gather(w_fc, 'shard', axis=0, tiled=True)]
    reduce_scatter x1, waiting for transfers between devices: 26 us -> 12.3 us  [on_device(): lax.psum_scatter(d_key_terms.reshape(block, local_width).astype(jnp.bfloa...]
    reduce_scatter x1, waiting for transfers between devices: 13.5 us -> 25.4 us  [on_device(): lax.psum_scatter(d_value_terms.reshape(block, local_width).astype(jnp.bfl...]
    dynamic_update_slice x12, local copies, waits for them, and re-layouts: 8.3 us -> 18.7 us  [on_device(): lax.scan(back_piece, zero_query, (key_blocks, value_blocks, starts))]
  transfers between devices with their start and end apart: 16 -> 18, of which waited for: 16 -> 16; matrix products, arithmetic and copies ran while one was open for 8% -> 9% of each run, Pallas kernels for 0% -> 0%
where the time goes in v1:
time: 813 us; the launch traced here: 811 us
  waiting for transfers between devices  543 us (67%)
  matrix products  90.9 us (11%)
  blocking collectives  82.1 us (10%)
  local copies, waits for them, and re-layouts  38.3 us (5%)
  other arithmetic  29.9 us (4%)
  between operations  14.4 us (2%)
    ppermute x2, waiting for transfers between devices, build_slot(): local_out = lax.ppermute(block_now, named_axis, low)  99.4 us
    psum x1, blocking collectives, on_device(): lax.psum((g_bqv, g_bout, g_bfc, g_bproj, g_ln1g, g_ln1b, g_ln2g, g_ln2b),...  82.1 us
    reduce_scatter x1, waiting for transfers between devices, on_device(): lax.psum_scatter(g_proj.astype(jnp.bfloat16), 'shard', scatter_dimension=...  55.6 us
    reduce_scatter x1, waiting for transfers between devices, on_device(): lax.psum_scatter(g_fc.astype(jnp.bfloat16), 'shard', scatter_dimension=0,...  55.5 us
    dot_general x18, matrix products, dot32(): return jnp.dot(left, right, preferred_element_type=jnp.float32)  53 us
    reduce_scatter x1, waiting for transfers between devices, on_device(): lax.psum_scatter(g_qkv.astype(jnp.bfloat16), 'shard', scatter_dimension=1...  46.8 us
    all_gather x1, waiting for transfers between devices, on_device(): lax.all_gather(w_qkv, 'shard', axis=1, tiled=True)  45.8 us
    psum x1, waiting for transfers between devices, on_device(): lax.psum(part_qkv.astype(jnp.bfloat16), 'ctx').astype(jnp.float32)  39.9 us
  transfers between devices with their start and end apart: 18, of which 16 were waited for; matrix products, arithmetic and copies ran while one was open for 9% of the time, Pallas kernels for 0%

profile of v1, /device:TPU:0, one launch (start us, length us, event | category | flops | bytes accessed | tf_op | source)
XLA Modules:
  0.0 811.2 jit_solution(7591847104517518965)
XLA Ops:
  10.6 45.8 %all-gather.7.cloned.1.call-done = bf16[3,1024,512]{2,1,0:T(8,128)(2,1)} async-done(((bf16[3,256,512]{2,1,0:T(8,128)(2,1)}), bf16[3,1024,512]{2,1,0:T(8,128)(2,1)}) %all-gather.7.cloned.1.call-update) | async-done | bytes 3145744 | tf_op jit(solution)/shard_map/all_gather | solution.py:78
  56.4 2.6 convolution_convert_fusion.10
  59.2 2.4 fusion.55
  64.8 22.4 %all-gather.9.cloned.1.call-done = bf16[1024,512]{1,0:T(8,128)(2,1)} async-done(((bf16[256,512]{1,0:T(8,128)(2,1)}), bf16[1024,512]{1,0:T(8,128)(2,1)}) %all-gather.9.cloned.1.call-update) | async-done | bytes 1048592 | tf_op jit(solution)/shard_map/all_gather | solution.py:95
  88.7 28.1 %all-gather.11.cloned.1.call-done = bf16[1024,512]{1,0:T(8,128)(2,1)} async-done(((bf16[256,512]{1,0:T(8,128)(2,1)}), bf16[1024,512]{1,0:T(8,128)(2,1)}) %all-gather.11.cloned.1.call-update) | async-done | bytes 1048592 | tf_op jit(solution)/shard_map/all_gather | solution.py:96
  118.2 2.1 fusion.21
  121.7 22.5 %all-gather.13.cloned.1.call-done = bf16[512,1024]{1,0:T(8,128)(2,1)} async-done(((bf16[512,256]{1,0:T(8,128)(2,1)}), bf16[512,1024]{1,0:T(8,128)(2,1)}) %all-gather.13.cloned.1.call-update) | async-done | bytes 1048592 | tf_op jit(solution)/shard_map/all_gather | solution.py:79
  144.2 2.6 convolution_convert_fusion.6
  149.9 23.3 %collective-permute-done = bf16[256,2048]{1,0:T(8,128)(2,1)S(1)} collective-permute-done((bf16[256,2048]{1,0:T(8,128)(2,1)S(1)}, bf16[256,2048]{1,0:T(8,128)(2,1)S(1)}, u32[]{:S(2)}, u32[]{:S(2)}) %collective-permute-start) | collective-permute-done | bytes 1048608 | tf_op jit(solution)/shard_map/ppermute | solution.py:70
  173.2 2.3 maximum_select_fusion.4
  179.8 76.1 %collective-permute-done.1 = bf16[512,2048]{1,0:T(8,128)(2,1)} collective-permute-done((bf16[512,2048]{1,0:T(8,128)(2,1)}, bf16[512,2048]{1,0:T(8,128)(2,1)}, u32[]{:S(2)}, u32[]{:S(2)}) %collective-permute-start.1) | collective-permute-done | bytes 2097184 | tf_op jit(solution)/shard_map/ppermute | solution.py:70
  255.9 6.5 fusion.34
  262.4 8.0 fusion.95
  270.4 38.4 %all-gather.17.cloned.1.call-done = bf16[1024,2048]{1,0:T(8,128)(2,1)} async-done(((bf16[256,2048]{1,0:T(8,128)(2,1)}), bf16[1024,2048]{1,0:T(8,128)(2,1)}) %all-gather.17.cloned.1.call-update) | async-done | bytes 4194320 | tf_op jit(solution)/shard_map/all_gather | solution.py:126
  308.8 4.3 convolution_convert_fusion.7
  313.4 2.8 reshape.279
  316.2 1.9 copy.62
  318.2 2.8 reshape.278
  321.0 1.9 copy.61
  322.9 8.9 %all-reduce.10.cloned.1.call-done = bf16[256,1024]{1,0:T(8,128)(2,1)} async-done(((bf16[256,1024]{1,0:T(8,128)(2,1)}), bf16[256,1024]{1,0:T(8,128)(2,1)}) %all-reduce.10.cloned.1.call-update) | async-done | bytes 524304 | tf_op jit(solution)/shard_map/psum | solution.py:138
  338.3 67.0 %while.15 = (s32[]{:T(128)}, f32[256,8,64]{0,2,1:T(8,128)}, bf16[4,256,512]{2,1,0:T(8,128)(2,1)}, bf16[4,256,512]{2,1,0:T(8,128)(2,1)}, bf16[4,256,8,64]{1,3,2,0...) while((s32[]{:T(128)}, f32[256,8,64]{0,2,1:T(8,128)}, ...), condition=%wide.region_13.14_spmd.clone, body=%wide.region_12.13_spmd.clone.sunk | while | flops 340197888 | bytes 15174041 | solution.py:172
  346.1 1.8 copy.106
  347.9 2.1 fusion.154
  352.9 2.0 fusion.153
  362.7 1.8 copy.106
  364.5 2.1 fusion.154
  369.5 2.2 fusion.153
  379.5 1.8 copy.106
  381.3 2.1 fusion.154
  386.3 2.2 fusion.153
  396.3 1.8 copy.106
  398.1 2.1 fusion.154
  403.1 2.2 fusion.153
  408.0 4.6 convolution_convert_fusion.1
  413.7 5.2 convolution_convert_fusion
  421.7 12.3 %reduce-scatter.7.cloned.1.call-done = bf16[256,512]{1,0:T(8,128)(2,1)} async-done(((bf16[1024,512]{1,0:T(8,128)(2,1)}), bf16[256,512]{1,0:T(8,128)(2,1)}) %reduce-scatter.7.cloned.1.call-update) | async-done | bytes 262160 | tf_op jit(solution)/shard_map/reduce_scatter | solution.py:176
  434.0 2.5 fusion.45
  436.5 25.4 %reduce-scatter.9.cloned.1.call-done = bf16[256,512]{1,0:T(8,128)(2,1)} async-done(((bf16[1024,512]{1,0:T(8,128)(2,1)}), bf16[256,512]{1,0:T(8,128)(2,1)}) %reduce-scatter.9.cloned.1.call-update) | async-done | bytes 262160 | tf_op jit(solution)/shard_map/reduce_scatter | solution.py:182
  463.7 2.0 pad_maximum_fusion
  465.7 5.2 convolution_convert_fusion.8
  474.2 17.1 %reduce-scatter.13.cloned.1.call-done = bf16[512,256]{1,0:T(8,128)(2,1)} async-done(((bf16[512,1024]{1,0:T(8,128)(2,1)}), bf16[512,256]{1,0:T(8,128)(2,1)}) %reduce-scatter.13.cloned.1.call-update) | async-done | bytes 262160 | tf_op jit(solution)/shard_map/reduce_scatter | solution.py:210
  491.3 55.5 %reduce-scatter.15.cloned.1.call-done = bf16[256,2048]{1,0:T(8,128)(2,1)} async-done(((bf16[1024,2048]{1,0:T(8,128)(2,1)}), bf16[256,2048]{1,0:T(8,128)(2,1)}) %reduce-scatter.15.cloned.1.call-update) | async-done | bytes 1048592 | tf_op jit(solution)/shard_map/reduce_scatter | solution.py:213
  546.7 55.6 %reduce-scatter.17.cloned.1.call-done = bf16[2048,256]{1,0:T(8,128)(2,1)} async-done(((bf16[2048,1024]{1,0:T(8,128)(2,1)}), bf16[2048,256]{1,0:T(8,128)(2,1)}) %reduce-scatter.17.cloned.1.call-update) | async-done | bytes 1048592 | tf_op jit(solution)/shard_map/reduce_scatter | solution.py:216
  602.3 46.8 %reduce-scatter.11.cloned.1.call-done = bf16[3,256,512]{2,1,0:T(8,128)(2,1)} async-done(((bf16[3,1024,512]{2,1,0:T(8,128)(2,1)}), bf16[3,256,512]{2,1,0:T(8,128)(2,1)}) %reduce-scatter.11.cloned.1.call-update) | async-done | bytes 786448 | tf_op jit(solution)/shard_map/reduce_scatter | solution.py:207
  649.3 22.2 %all-reduce.14.cloned.1.call-done = (bf16[256,1024]{1,0:T(8,128)(2,1)}, bf16[256,1024]{1,0:T(8,128)(2,1)}) async-done(((bf16[256,1024]{1,0:T(8,128)(2,1)}, bf16[256,1024]{1,0:T(8,128)(2,1)}), (bf16[256,1024]{1,0:T(8,128)(2,1)}, bf16[256,1024]{1,0:T(8,128)(2,1)})) %all-reduce.14.cloned.1.call-update) | async-done | bytes 1048592 | tf_op jit(solution)/shard_map/psum | solution.py:121
  674.6 82.1 %all-reduce = (f32[2,512]{1,0:T(2,128)}, f32[1024]{0:T(1024)}, f32[2048]{0:T(1024)}, f32[1024]{0:T(1024)}, f32[1024]{0:T(1024)}, /*index=5*/f32[1024]{0:T(1024)}, f32[1024]{0:T(1024)}, f32[1024]{0:T(1024)}) all-reduce(f32[2,512]{1,0:T(2,128)S(1)} %pad_maximum_fusion.1, ...), channel_id=1, replica_groups=mesh['shard'=4,'ctx'=4,'tp'=2] {'shard','ctx'}, use_global_device_ids=true, to_apply=%region_29.30 | all-reduce | flops 9216 | bytes 73728 | tf_op jit(solution)/shard_map/psum | solution.py:226
  758.3 39.9 %all-reduce.12.cloned.1.call-done = (bf16[3,256,512]{2,1,0:T(8,128)(2,1)}, bf16[512,256]{1,0:T(8,128)(2,1)}, bf16[256,2048]{1,0:T(8,128)(2,1)}, bf16[2048,256]{1,0:T(8,128)(2,1)}) async-done(((bf16[3,256,512]{2,1,0:T(8,128)(2,1)}, bf16[512,256]{1,0:T(8,128)(2,1)}, bf16[256,2048]{1,0:T(8,128)(2,1)}, bf16[2048,256]{1,0:T(8,128)(2,1)}), (bf16[3,256,512]{2,1,0:T(8,128)(2,1)}, bf16[512,256]{1,0:T(8,128)(2,1)}, ...) | async-done | bytes 3145744 | tf_op jit(solution)/shard_map/psum | solution.py:221
  798.1 2.9 convert_element_type.172
  (216 shorter events, 79.5 us)
Async XLA Ops:
  7.2 49.3 %all-gather.7.cloned.1.call-start = ((), (), s32[]{:S(2)}) async-start(), calls=%async_computation.6 | async-start | bytes 3932160 | tf_op jit(solution)/shard_map/all_gather | solution.py:78
  7.9 79.3 %all-gather.9.cloned.1.call-start = ((), (), s32[]{:S(2)}) async-start(), calls=%async_computation.7 | async-start | bytes 1310720 | tf_op jit(solution)/shard_map/all_gather | solution.py:95
  9.2 50.0 %copy-start.32 = (f32[2,512]{1,0:T(2,128)S(1)}, f32[2,512]{1,0:T(2,128)}, u32[]{:S(2)}) copy-start(f32[2,512]{1,0:T(2,128)} %param.24) | copy-start | bytes 12292
  9.2 50.0 %copy-start = (bf16[256,1024]{1,0:T(8,128)(2,1)S(1)}, bf16[256,1024]{1,0:T(8,128)(2,1)}, u32[]{:S(2)}) copy-start(bf16[256,1024]{1,0:T(8,128)(2,1)} %param.17) | copy-start | bytes 1572868
  9.2 50.0 %copy-start.30 = (f32[1024]{0:T(1024)S(1)}, f32[1024]{0:T(1024)}, u32[]{:S(2)}) copy-start(f32[1024]{0:T(1024)} %param.28) | copy-start | bytes 12292
  9.2 50.0 %copy-start.35 = (f32[1024]{0:T(1024)S(1)}, f32[1024]{0:T(1024)}, u32[]{:S(2)}) copy-start(f32[1024]{0:T(1024)} %param.29) | copy-start | bytes 12292
  59.1 3.2 copy-start.36
  59.1 57.7 %all-gather.11.cloned.1.call-start = ((), (), s32[]{:S(2)}) async-start(), calls=%async_computation.8 | async-start | bytes 1310720 | tf_op jit(solution)/shard_map/all_gather | solution.py:96
  61.6 82.6 %all-gather.13.cloned.1.call-start = ((), (), s32[]{:S(2)}) async-start(), calls=%async_computation.9 | async-start | bytes 1310720 | tf_op jit(solution)/shard_map/all_gather | solution.py:79
  62.2 114.8 %all-reduce.8.cloned.1.call-start = ((), (), s32[]{:S(2)}) async-start(), calls=%async_computation.10 | async-start | bytes 1048576 | tf_op jit(solution)/shard_map/psum | solution.py:116
  121.7 26.4 %copy-start.12 = (bf16[256,8,64]{0,2,1:T(8,128)(2,1)}, bf16[256,8,64]{0,2,1:T(8,128)(2,1)S(1)}, u32[]{:S(2)}) copy-start(bf16[256,8,64]{0,2,1:T(8,128)(2,1)S(1)} %fusion.70) | copy-start | bytes 786436
  144.2 4.2 copy-start.9
  146.8 115.6 %all-gather.15.cloned.1.call-start = ((), (), s32[]{:S(2)}) async-start(), calls=%async_computation.11 | async-start | bytes 5242880 | tf_op jit(solution)/shard_map/all_gather | solution.py:81
  147.4 161.4 %all-gather.17.cloned.1.call-start = ((), (), s32[]{:S(2)}) async-start(), calls=%async_computation.12 | async-start | bytes 5242880 | tf_op jit(solution)/shard_map/all_gather | solution.py:126
  148.2 183.7 %all-reduce.10.cloned.1.call-start = ((), (), s32[]{:S(2)}) async-start(), calls=%async_computation.13 | async-start | bytes 1048576 | tf_op jit(solution)/shard_map/psum | solution.py:138
  148.4 24.8 %collective-permute-start = (bf16[256,2048]{1,0:T(8,128)(2,1)S(1)}, bf16[256,2048]{1,0:T(8,128)(2,1)S(1)}, u32[]{:S(2)}, u32[]{:S(2)}) collective-permute-start(bf16[256,2048]{1,0:T(8,128)(2,1)S(1)} %copy-done.9), channel_id=1, source_target_pairs={{0,8},{8,0},{16,24},{24,16},{1,9},{9,1},{17,25},{25,17},{2,10},{10... | collective-permute-start | bytes 3145736 | tf_op jit(solution)/shard_map/ppermute | solution.py:70
  149.9 27.1 %copy-start.25 = (f32[1024]{0:T(1024)S(1)}, f32[1024]{0:T(1024)}, u32[]{:S(2)}) copy-start(f32[1024]{0:T(1024)} %param.25) | copy-start | bytes 12292
  175.5 80.4 %copy-start.28 = (f32[1024]{0:T(1024)S(1)}, f32[1024]{0:T(1024)}, u32[]{:S(2)}) copy-start(f32[1024]{0:T(1024)} %param.30) | copy-start | bytes 12292
  175.5 80.4 %copy-start.29 = (f32[1024]{0:T(1024)S(1)}, f32[1024]{0:T(1024)}, u32[]{:S(2)}) copy-start(f32[1024]{0:T(1024)} %param.31) | copy-start | bytes 12292
  175.5 80.4 %copy-start.34 = (f32[2048]{0:T(1024)S(1)}, f32[2048]{0:T(1024)}, u32[]{:S(2)}) copy-start(f32[2048]{0:T(1024)} %param.26) | copy-start | bytes 24580
  175.5 80.4 %collective-permute-start.1 = (bf16[512,2048]{1,0:T(8,128)(2,1)}, bf16[512,2048]{1,0:T(8,128)(2,1)}, u32[]{:S(2)}, u32[]{:S(2)}) collective-permute-start(bf16[512,2048]{1,0:T(8,128)(2,1)} %maximum_select_fusion.4), channel_id=1, source_target_pairs={{0,16},{8,24},{16,0},{24,8},{1,17},{9,25},{17,1},{25,9},{2,18},{10... | collective-permute-start | bytes 6291464 | tf_op jit(solution)/shard_map/ppermute | solution.py:70
  177.0 78.9 %copy-start.2 = (bf16[256,1024]{1,0:T(8,128)(2,1)S(1)}, bf16[256,1024]{1,0:T(8,128)(2,1)}, u32[]{:S(2)}) copy-start(bf16[256,1024]{1,0:T(8,128)(2,1)} %all-reduce.8.cloned.1.call-done) | copy-start | bytes 1572868
  179.8 82.7 %copy-start.21 = (bf16[256,1024]{1,0:T(8,128)(2,1)S(1)}, bf16[256,1024]{1,0:T(8,128)(2,1)}, u32[]{:S(2)}) copy-start(bf16[256,1024]{1,0:T(8,128)(2,1)} %param.19) | copy-start | bytes 1572868
  270.4 42.7 %copy-start.19 = (bf16[256,2048]{1,0:T(8,128)(2,1)}, bf16[256,2048]{1,0:T(8,128)(2,1)S(1)}, u32[]{:S(2)}) copy-start(bf16[256,2048]{1,0:T(8,128)(2,1)S(1)} %get-tuple-element.232) | copy-start | bytes 3145732
  313.1 120.9 %reduce-scatter.7.cloned.1.call-start = ((), (), s32[]{:S(2)}) async-start(), calls=%async_computation.14 | async-start | bytes 1310720 | tf_op jit(solution)/shard_map/reduce_scatter | solution.py:176
  322.9 12.3 %copy-start.22 = (bf16[256,1024]{1,0:T(8,128)(2,1)S(1)}, bf16[256,1024]{1,0:T(8,128)(2,1)}, u32[]{:S(2)}) copy-start(bf16[256,1024]{1,0:T(8,128)(2,1)} %param.19) | copy-start | bytes 1572868
  331.9 3.4 copy-start.7
  338.3 3.3 copy-start.37
  350.0 4.9 copy-start.38
  355.0 3.3 copy-start.37
  366.6 5.1 copy-start.38
  371.7 3.3 copy-start.37
  383.4 5.1 copy-start.38
  388.5 3.3 copy-start.37
  400.2 5.1 copy-start.38
  405.3 56.6 %reduce-scatter.9.cloned.1.call-start = ((), (), s32[]{:S(2)}) async-start(), calls=%async_computation.15 | async-start | bytes 1310720 | tf_op jit(solution)/shard_map/reduce_scatter | solution.py:182
  405.9 85.4 %reduce-scatter.13.cloned.1.call-start = ((), (), s32[]{:S(2)}) async-start(), calls=%async_computation.17 | async-start | bytes 1310720 | tf_op jit(solution)/shard_map/reduce_scatter | solution.py:210
  408.0 138.7 %reduce-scatter.15.cloned.1.call-start = ((), (), s32[]{:S(2)}) async-start(), calls=%async_computation.18 | async-start | bytes 5242880 | tf_op jit(solution)/shard_map/reduce_scatter | solution.py:213
  412.7 189.6 %reduce-scatter.17.cloned.1.call-start = ((), (), s32[]{:S(2)}) async-start(), calls=%async_computation.19 | async-start | bytes 5242880 | tf_op jit(solution)/shard_map/reduce_scatter | solution.py:216
  418.9 230.2 %reduce-scatter.11.cloned.1.call-start = ((), (), s32[]{:S(2)}) async-start(), calls=%async_computation.16 | async-start | bytes 3932160 | tf_op jit(solution)/shard_map/reduce_scatter | solution.py:207
  465.7 205.8 %all-reduce.14.cloned.1.call-start = ((), (), s32[]{:S(2)}) async-start(), calls=%async_computation.21 | async-start | bytes 2097152 | tf_op jit(solution)/shard_map/psum | solution.py:121
  465.7 5.2 copy-start.11
  474.1 324.0 %all-reduce.12.cloned.1.call-start = ((), (), s32[]{:S(2)}) async-start(), calls=%async_computation.20 | async-start | bytes 6291456 | tf_op jit(solution)/shard_map/psum | solution.py:221
  649.1 25.5 %copy-start.31 = (f32[2048]{0:T(1024)S(1)}, f32[2048]{0:T(1024)}, u32[]{:S(2)}) copy-start(f32[2048]{0:T(1024)} %get-tuple-element.231) | copy-start | bytes 24580
  649.1 107.6 %copy-start.33 = (f32[1024]{0:T(1024)S(1)}, f32[1024]{0:T(1024)}, u32[]{:S(2)}) copy-start(f32[1024]{0:T(1024)} %param.27) | copy-start | bytes 12292
  671.4 85.3 %copy-start.8 = (bf16[256,1024]{1,0:T(8,128)(2,1)S(1)}, bf16[256,1024]{1,0:T(8,128)(2,1)}, u32[]{:S(2)}) copy-start(bf16[256,1024]{1,0:T(8,128)(2,1)} %get-tuple-element.230) | copy-start | bytes 1572868
  671.5 85.3 %copy-start.24 = (bf16[256,1024]{1,0:T(8,128)(2,1)S(1)}, bf16[256,1024]{1,0:T(8,128)(2,1)}, u32[]{:S(2)}) copy-start(bf16[256,1024]{1,0:T(8,128)(2,1)} %get-tuple-element.229) | copy-start | bytes 1572868
  798.1 2.9 copy-start.15
  (15 other events, 25.8 us)
Sparse Core Ops, SparseCore 0:
  9.8 46.5 all-gather.6
  59.2 27.9 all-gather.8
  89.4 27.3 all-gather.10
  118.4 25.7 all-gather.12
  147.0 18.5 all-reduce.7
  167.3 87.0 all-gather.14
  256.2 52.5 all-gather.16
  313.2 18.5 all-reduce.9
  405.4 28.4 reduce-scatter.6
  436.1 25.7 reduce-scatter.8
  464.8 26.4 reduce-scatter.12
  494.1 52.5 reduce-scatter.14
  549.7 52.5 reduce-scatter.16
  605.2 43.8 reduce-scatter.10
  651.9 19.5 all-reduce.13
  673.9 124.1 all-reduce.11
